TPU v7x, 32 devices: a whole 2x2x4 slice. The times are simulated.
32 devices in a mesh: snap: 2 (over y), row: 4 (over z), col: 4 (over x, core).
Axes of the slice: x: 2, y: 2, z: 4, core: 2. Of those that a mesh axis runs over, the one named last changes fastest.
Arguments:
- orbitals: float32 [12288, 768], P(('snap', 'row', 'col')), parts along dimension 0, may hold values from -6 to 6
- screened: float32 [6, 6144, 6144], P('snap', 'row', 'col'), parts along dimension 0, may hold values from -0.0029296875 to 0.0029296875
- green_weight: float32 [6, 768], P('snap'), parts along dimension 0, may hold values from 0.05 to 1
- time_weight: float32 [3], replicated, may hold values from 0.3 to 1
Outputs:
- updated: float32 [12288, 768], P(('snap', 'row', 'col')), parts along dimension 0
There are 2 independent parts, one for each index of `snap`. A program takes and returns all parts, laid end to end along the dimension named above; an argument that names none is the same for every part. Nothing has to cross between parts.
All inputs are finite; a program needn't handle non-finite values.
Results may differ from a plain program's by a relative error of at most 0.00013.
Values sent between devices are 32-bit elements; how exact they have to be, the bound alone decides.
A program may use at most 128 MiB of HBM per device.

v0:
```python
import functools

import jax
import jax.numpy as jnp
from jax import lax
from jax.experimental import pallas as pl
from jax.experimental.pallas import tpu as pltpu
from jax.sharding import PartitionSpec as P

PASSES = 2


def split(value):
    high = value.astype(jnp.bfloat16)
    low = (value - high.astype(jnp.float32)).astype(jnp.bfloat16)
    return high, low


def apply_kernel(times, parts, has_total, index_ref, *refs):
    rows_refs, refs = refs[:parts], refs[parts:]
    cols_refs, refs = refs[:parts], refs[parts:]
    weight_ref, screened_ref, refs = refs[0], refs[1], refs[2:]
    total_refs = None
    if has_total:
        total_refs, refs = refs[:parts], refs[parts:]
    out_refs, (weighted, plain) = refs[:parts], refs[parts:]

    @pl.when(pl.program_id(0) == 0)
    def _():
        cols = jnp.concatenate([ref[...] for ref in cols_refs], axis=1)
        width, depth = cols.shape
        high, low = split(cols)
        plain[0:width, :] = high
        plain[width : 2 * width, :] = high
        plain[2 * width : 3 * width, :] = low
        for t in range(times):
            high, low = split((cols * weight_ref[t : t + 1, :]).T)
            weighted[t, 0:depth, :] = high
            weighted[t, depth : 2 * depth, :] = high
            weighted[t, 2 * depth : 3 * depth, :] = low

    high, low = split(jnp.concatenate([ref[...] for ref in rows_refs], axis=1))
    rows = jnp.concatenate([high, low, high], axis=1)
    mixed = None
    for t in range(times):
        green = jnp.dot(rows, weighted[t], preferred_element_type=jnp.float32)
        term = green * screened_ref[t]
        mixed = term if mixed is None else mixed + term
    high, low = split(mixed)
    mixed = jnp.concatenate([high, low, high], axis=1)
    applied = jnp.dot(mixed, plain[...], preferred_element_type=jnp.float32)
    part = applied.shape[1] // parts
    for k in range(parts):
        value = applied[:, k * part : (k + 1) * part]
        out_refs[k][...] = value + total_refs[k][...] if has_total else value


def apply_block(index, rows, cols, weight, screened, total):
    times = screened.shape[0]
    parts = len(rows)
    n_rows, part = rows[0].shape
    depth = parts * part
    width = cols[0].shape[0]
    tile = next(k for k in (512, 384, 256, 128, n_rows) if n_rows % k == 0)
    row_spec = pl.BlockSpec((tile, part), lambda i, ix: (i, 0))
    in_specs = [row_spec] * parts
    in_specs += [pl.BlockSpec((width, part), lambda i, ix: (0, 0))] * parts
    in_specs += [
        pl.BlockSpec((times, depth), lambda i, ix: (0, 0)),
        pl.BlockSpec((times, tile, width), lambda i, ix: (0, i, ix[0])),
    ]
    args = [index, *rows, *cols, weight, screened]
    if total is not None:
        in_specs += [row_spec] * parts
        args += total
    return pl.pallas_call(
        functools.partial(apply_kernel, times, parts, total is not None),
        out_shape=[jax.ShapeDtypeStruct((n_rows, part), jnp.float32)] * parts,
        grid_spec=pltpu.PrefetchScalarGridSpec(
            num_scalar_prefetch=1,
            grid=(n_rows // tile,),
            in_specs=in_specs,
            out_specs=[row_spec] * parts,
            scratch_shapes=[
                pltpu.VMEM((times, 3 * depth, width), jnp.bfloat16),
                pltpu.VMEM((3 * width, depth), jnp.bfloat16),
            ],
        ),
        compiler_params=pltpu.CompilerParams(
            dimension_semantics=("arbitrary",), vmem_limit_bytes=56 * 1024 * 1024
        ),
        cost_estimate=pl.CostEstimate(
            flops=6 * (times + 1) * n_rows * width * depth,
            bytes_accessed=4 * (times * n_rows * width + 3 * n_rows * depth),
            transcendentals=0,
        ),
    )(*args)


def scatter_rows(value):
    n_col = lax.axis_size("col")
    if n_col & (n_col - 1):
        return lax.psum_scatter(value, "col", scatter_dimension=0, tiled=True)
    me = lax.axis_index("col")
    points = value.shape[0] // n_col
    value = value.reshape(n_col, points, value.shape[1])
    distance = 1
    while distance < n_col:
        bit = (me // distance) % 2
        pairs = value.reshape((value.shape[0] // 2, 2) + value.shape[1:])
        mine = lax.dynamic_index_in_dim(pairs, bit, 1, keepdims=False)
        theirs = lax.dynamic_index_in_dim(pairs, 1 - bit, 1, keepdims=False)
        swap = [(k, k ^ distance) for k in range(n_col)]
        value = mine + lax.ppermute(theirs, "col", swap)
        distance *= 2
    return value[0]


def body(orbitals, screened, green_weight, time_weight):
    n_row = lax.axis_size("row")
    n_col = lax.axis_size("col")
    factor = n_col // n_row
    points, depth = orbitals.shape
    weight = green_weight * time_weight[:, None]
    to_columns = [
        ((c // factor) * n_col + (c % factor) * n_row + m, m * n_col + c)
        for m in range(n_row)
        for c in range(n_col)
    ]
    ring = [(k, (k + 1) % n_row) for k in range(n_row)]
    me = lax.axis_index("row")
    parts = 1
    own = jnp.split(orbitals, parts, axis=1)
    for step in range(PASSES):
        piece = [lax.ppermute(o, ("row", "col"), to_columns) for o in own]
        rows = [lax.all_gather(o, "col", axis=0, tiled=True) for o in own]
        total = None
        if points % 128 == 0:
            for hop in range(n_row):
                later = None
                if hop < n_row - 1:
                    if total is not None:
                        piece, total = lax.optimization_barrier((piece, total))
                    later = [lax.ppermute(p, "row", ring) for p in piece]
                index = lax.rem(me - hop + n_row, n_row).astype(jnp.int32).reshape(1)
                total = apply_block(index, rows, piece, weight, screened, total)
                piece = later
        else:
            columns = [lax.all_gather(p, "row", axis=0, tiled=True) for p in piece]
            index = jnp.zeros((1,), jnp.int32)
            total = apply_block(index, rows, columns, weight, screened, None)
        own = [
            o - scatter_rows(v)
            for o, v in zip(own, total)
        ]
    return jnp.concatenate(own, axis=1)


def solution(mesh):
    in_specs = (P(("snap", "row", "col"), None), P("snap", "row", "col"), P("snap", None), P())
    out_specs = P(("snap", "row", "col"), None)
    return jax.shard_map(body, mesh=mesh, in_specs=in_specs, out_specs=out_specs, check_vma=False)
```

profile of v0, /device:TPU:0, one launch (start us, length us, event | category | flops | bytes accessed | tf_op | source)
XLA Modules:
  0.0 462.0 jit_solution(7167257660921477261)
XLA Ops:
  7.3 1.9 collective-permute-start
  9.2 26.9 %collective-permute-start.1 = (f32[384,768]{1,0:T(8,128)S(1)}, f32[384,768]{1,0:T(8,128)S(1)}, u32[]{:S(2)}, u32[]{:S(2)}) collective-permute-start(f32[384,768]{1,0:T(8,128)S(1)} %collective-permute-done.refs_1_), channel_id=1, source_target_pairs={{0,4},{4,8},{8,12},{12,0},{1,5},{5,9},{9,13},{13,1},{2,6},{6,10},{... | collective-permute-start | bytes 3538952 | tf_op jit(solution)/shard_map/ppermute | solution.py:144
  36.1 1.4 broadcast_multiply_fusion.refs_2_
  37.5 21.1 %all-gather.3.cloned.1.call-done.refs_0_ = f32[1536,768]{1,0:T(8,128)} async-done(((f32[384,768]{1,0:T(8,128)}), f32[1536,768]{1,0:T(8,128)}) %all-gather.3.cloned.1.call-update) | async-done | bytes 4718608 | tf_op jit(solution)/shard_map/all_gather | solution.py:136
  58.6 20.9 %shard_map.46.refs_4_ = f32[1536,768]{1,0:T(8,128)} custom-call(s32[1]{0:T(128)} %bitcast.1.index_ref, f32[1536,768]{1,0:T(8,128)} %all-gather.3.cloned.1.call-done.refs_0_, f32[384,768]{1,0:T(8,128)} %copy-done.9, f32[3,768]{1,0:T(4,128)} %broadcast_multiply_fusion.refs_2_, f32[3,1536,1536]{2,1,0:T(8,128)} %refs_3_.15), custom_call_target="tpu_custom_call" | custom-call | flops 10871635968 | bytes 21233664 | tf_op jit(solution)/shard_map/pallas_call | solution.py:76
  79.5 37.5 %collective-permute-start.2 = (f32[384,768]{1,0:T(8,128)S(1)}, f32[384,768]{1,0:T(8,128)S(1)}, u32[]{:S(2)}, u32[]{:S(2)}) collective-permute-start(f32[384,768]{1,0:T(8,128)S(1)} %collective-permute-done.1.refs_1_), channel_id=1, source_target_pairs={{0,4},{4,8},{8,12},{12,0},{1,5},{5,9},{9,13},{13,1},{2,6},{6,10},{... | collective-permute-start | bytes 3538952 | tf_op jit(solution)/shard_map/ppermute | solution.py:144
  116.9 21.4 %shard_map.47.refs_4_ = f32[1536,768]{1,0:T(8,128)} custom-call(s32[1]{0:T(128)} %bitcast.2.index_ref, f32[1536,768]{1,0:T(8,128)} %all-gather.3.cloned.1.call-done.refs_0_, f32[384,768]{1,0:T(8,128)} %copy-done.5, f32[3,768]{1,0:T(4,128)} %broadcast_multiply_fusion.refs_2_, f32[3,1536,1536]{2,1,0:T(8,128)} %refs_3_.15, f32[1536,768]{1,0:T(8,128)} %shard_map.46.refs_4_), custom_call_target="tpu_custom_call" | custom-call | flops 10871635968 | bytes 21233664 | tf_op jit(solution)/shard_map/pallas_call | solution.py:76
  138.4 5.4 %collective-permute-done.2.refs_1_ = f32[384,768]{1,0:T(8,128)S(1)} collective-permute-done((f32[384,768]{1,0:T(8,128)S(1)}, f32[384,768]{1,0:T(8,128)S(1)}, u32[]{:S(2)}, u32[]{:S(2)}) %collective-permute-start.2) | collective-permute-done | bytes 1179680 | tf_op jit(solution)/shard_map/ppermute | solution.py:144
  144.8 21.3 %shard_map.48.refs_4_ = f32[1536,768]{1,0:T(8,128)} custom-call(s32[1]{0:T(128)} %bitcast.3.index_ref, f32[1536,768]{1,0:T(8,128)} %all-gather.3.cloned.1.call-done.refs_0_, f32[384,768]{1,0:T(8,128)} %copy-done.3, f32[3,768]{1,0:T(4,128)} %broadcast_multiply_fusion.refs_2_, f32[3,1536,1536]{2,1,0:T(8,128)} %refs_3_.15, f32[1536,768]{1,0:T(8,128)} %shard_map.47.refs_4_), custom_call_target="tpu_custom_call" | custom-call | flops 10871635968 | bytes 21233664 | tf_op jit(solution)/shard_map/pallas_call | solution.py:76
  166.2 6.0 %collective-permute-done.3.refs_1_ = f32[384,768]{1,0:T(8,128)S(1)} collective-permute-done((f32[384,768]{1,0:T(8,128)S(1)}, f32[384,768]{1,0:T(8,128)S(1)}, u32[]{:S(2)}, u32[]{:S(2)}) %collective-permute-start.3) | collective-permute-done | bytes 1179680 | tf_op jit(solution)/shard_map/ppermute | solution.py:144
  173.2 21.4 %shard_map.49 = f32[1536,768]{1,0:T(8,128)} custom-call(s32[1]{0:T(128)} %bitcast.index_ref, f32[1536,768]{1,0:T(8,128)} %all-gather.3.cloned.1.call-done.refs_0_, f32[384,768]{1,0:T(8,128)} %copy-done.4, f32[3,768]{1,0:T(4,128)} %broadcast_multiply_fusion.refs_2_, f32[3,1536,1536]{2,1,0:T(8,128)} %refs_3_.15, f32[1536,768]{1,0:T(8,128)} %shard_map.48.refs_4_), custom_call_target="tpu_custom_call" | custom-call | flops 10871635968 | bytes 21233664 | tf_op jit(solution)/shard_map/pallas_call | solution.py:76
  194.6 1.8 dynamic-slice_bitcast_fusion.1
  196.5 4.6 collective-permute-done.4
  201.1 2.7 bitcast_add_fusion.1
  203.8 1.1 constant_dynamic-slice_fusion.1
  204.9 28.3 %collective-permute-done.5 = f32[1,384,768]{2,1,0:T(8,128)} collective-permute-done((f32[1,384,768]{2,1,0:T(8,128)}, f32[1,384,768]{2,1,0:T(8,128)}, u32[]{:S(2)}, u32[]{:S(2)}) %collective-permute-start.5) | collective-permute-done | bytes 1179680 | tf_op jit(solution)/shard_map/ppermute | solution.py:114
  233.3 2.5 bitcast_subtract_fusion.1
  235.8 1.9 collective-permute-start.6
  237.7 29.2 %collective-permute-start.7 = (f32[384,768]{1,0:T(8,128)S(1)}, f32[384,768]{1,0:T(8,128)S(1)}, u32[]{:S(2)}, u32[]{:S(2)}) collective-permute-start(f32[384,768]{1,0:T(8,128)S(1)} %collective-permute-done.6.refs_1_), channel_id=1, source_target_pairs={{0,4},{4,8},{8,12},{12,0},{1,5},{5,9},{9,13},{13,1},{2,6},{6,10},{... | collective-permute-start | bytes 3538952 | tf_op jit(solution)/shard_map/ppermute | solution.py:144
  266.9 16.1 %all-gather.5.cloned.1.call-done.refs_0_ = f32[1536,768]{1,0:T(8,128)} async-done(((f32[384,768]{1,0:T(8,128)}), f32[1536,768]{1,0:T(8,128)}) %all-gather.5.cloned.1.call-update) | async-done | bytes 4718608 | tf_op jit(solution)/shard_map/all_gather | solution.py:136
  283.0 21.0 %shard_map.50.refs_4_ = f32[1536,768]{1,0:T(8,128)} custom-call(s32[1]{0:T(128)} %bitcast.1.index_ref, f32[1536,768]{1,0:T(8,128)} %all-gather.5.cloned.1.call-done.refs_0_, f32[384,768]{1,0:T(8,128)} %copy-done.10, f32[3,768]{1,0:T(4,128)} %broadcast_multiply_fusion.refs_2_, f32[3,1536,1536]{2,1,0:T(8,128)} %refs_3_.15), custom_call_target="tpu_custom_call" | custom-call | flops 10871635968 | bytes 21233664 | tf_op jit(solution)/shard_map/pallas_call | solution.py:76
  304.0 36.2 %collective-permute-start.8 = (f32[384,768]{1,0:T(8,128)S(1)}, f32[384,768]{1,0:T(8,128)S(1)}, u32[]{:S(2)}, u32[]{:S(2)}) collective-permute-start(f32[384,768]{1,0:T(8,128)S(1)} %collective-permute-done.7.refs_1_), channel_id=1, source_target_pairs={{0,4},{4,8},{8,12},{12,0},{1,5},{5,9},{9,13},{13,1},{2,6},{6,10},{... | collective-permute-start | bytes 3538952 | tf_op jit(solution)/shard_map/ppermute | solution.py:144
  340.2 21.3 %shard_map.51.refs_4_ = f32[1536,768]{1,0:T(8,128)} custom-call(s32[1]{0:T(128)} %bitcast.2.index_ref, f32[1536,768]{1,0:T(8,128)} %all-gather.5.cloned.1.call-done.refs_0_, f32[384,768]{1,0:T(8,128)} %copy-done.6, f32[3,768]{1,0:T(4,128)} %broadcast_multiply_fusion.refs_2_, f32[3,1536,1536]{2,1,0:T(8,128)} %refs_3_.15, f32[1536,768]{1,0:T(8,128)} %shard_map.50.refs_4_), custom_call_target="tpu_custom_call" | custom-call | flops 10871635968 | bytes 21233664 | tf_op jit(solution)/shard_map/pallas_call | solution.py:76
  361.5 5.8 %collective-permute-done.8.refs_1_ = f32[384,768]{1,0:T(8,128)S(1)} collective-permute-done((f32[384,768]{1,0:T(8,128)S(1)}, f32[384,768]{1,0:T(8,128)S(1)}, u32[]{:S(2)}, u32[]{:S(2)}) %collective-permute-start.8) | collective-permute-done | bytes 1179680 | tf_op jit(solution)/shard_map/ppermute | solution.py:144
  368.3 21.4 %shard_map.52.refs_4_ = f32[1536,768]{1,0:T(8,128)} custom-call(s32[1]{0:T(128)} %bitcast.3.index_ref, f32[1536,768]{1,0:T(8,128)} %all-gather.5.cloned.1.call-done.refs_0_, f32[384,768]{1,0:T(8,128)} %copy-done.7, f32[3,768]{1,0:T(4,128)} %broadcast_multiply_fusion.refs_2_, f32[3,1536,1536]{2,1,0:T(8,128)} %refs_3_.15, f32[1536,768]{1,0:T(8,128)} %shard_map.51.refs_4_), custom_call_target="tpu_custom_call" | custom-call | flops 10871635968 | bytes 21233664 | tf_op jit(solution)/shard_map/pallas_call | solution.py:76
  389.8 6.2 %collective-permute-done.9.refs_1_ = f32[384,768]{1,0:T(8,128)S(1)} collective-permute-done((f32[384,768]{1,0:T(8,128)S(1)}, f32[384,768]{1,0:T(8,128)S(1)}, u32[]{:S(2)}, u32[]{:S(2)}) %collective-permute-start.9) | collective-permute-done | bytes 1179680 | tf_op jit(solution)/shard_map/ppermute | solution.py:144
  396.0 1.0 copy-done.8
  397.0 21.3 %shard_map.53 = f32[1536,768]{1,0:T(8,128)} custom-call(s32[1]{0:T(128)} %bitcast.index_ref, f32[1536,768]{1,0:T(8,128)} %all-gather.5.cloned.1.call-done.refs_0_, f32[384,768]{1,0:T(8,128)} %copy-done.8, f32[3,768]{1,0:T(4,128)} %broadcast_multiply_fusion.refs_2_, f32[3,1536,1536]{2,1,0:T(8,128)} %refs_3_.15, f32[1536,768]{1,0:T(8,128)} %shard_map.52.refs_4_), custom_call_target="tpu_custom_call" | custom-call | flops 10871635968 | bytes 21233664 | tf_op jit(solution)/shard_map/pallas_call | solution.py:76
  418.4 2.0 dynamic-slice_bitcast_fusion
  420.4 4.5 collective-permute-done.10
  425.4 28.0 %collective-permute-done.11 = f32[1,384,768]{2,1,0:T(8,128)S(1)} collective-permute-done((f32[1,384,768]{2,1,0:T(8,128)S(1)}, f32[1,384,768]{2,1,0:T(8,128)S(1)}, u32[]{:S(2)}, u32[]{:S(2)}) %collective-permute-start.11) | collective-permute-done | bytes 1179680 | tf_op jit(solution)/shard_map/ppermute | solution.py:114
  453.4 1.3 bitcast_subtract_fusion
  (37 shorter events, 4.4 us)
Async XLA Ops:
  6.5 52.1 %all-gather.3.cloned.1.call-start = ((), (), s32[]{:S(2)}) async-start(), calls=%async_computation | async-start | bytes 5898240 | tf_op jit(solution)/shard_map/all_gather | solution.py:136
  7.3 275.7 %all-gather.5.cloned.1.call-start = ((), (), s32[]{:S(2)}) async-start(), calls=%async_computation.1 | async-start | bytes 5898240 | tf_op jit(solution)/shard_map/all_gather | solution.py:136
  7.3 1.9 collective-permute-start
  9.2 49.4 %copy-start.9 = (f32[384,768]{1,0:T(8,128)}, f32[384,768]{1,0:T(8,128)S(1)}, u32[]{:S(2)}) copy-start(f32[384,768]{1,0:T(8,128)S(1)} %collective-permute-done.refs_1_) | copy-start | bytes 3538948
  9.2 70.2 %collective-permute-start.1 = (f32[384,768]{1,0:T(8,128)S(1)}, f32[384,768]{1,0:T(8,128)S(1)}, u32[]{:S(2)}, u32[]{:S(2)}) collective-permute-start(f32[384,768]{1,0:T(8,128)S(1)} %collective-permute-done.refs_1_), channel_id=1, source_target_pairs={{0,4},{4,8},{8,12},{12,0},{1,5},{5,9},{9,13},{13,1},{2,6},{6,10},{... | collective-permute-start | bytes 3538952 | tf_op jit(solution)/shard_map/ppermute | solution.py:144
  79.5 37.5 %copy-start.5 = (f32[384,768]{1,0:T(8,128)}, f32[384,768]{1,0:T(8,128)S(1)}, u32[]{:S(2)}) copy-start(f32[384,768]{1,0:T(8,128)S(1)} %collective-permute-done.1.refs_1_) | copy-start | bytes 3538948
  79.5 64.3 %collective-permute-start.2 = (f32[384,768]{1,0:T(8,128)S(1)}, f32[384,768]{1,0:T(8,128)S(1)}, u32[]{:S(2)}, u32[]{:S(2)}) collective-permute-start(f32[384,768]{1,0:T(8,128)S(1)} %collective-permute-done.1.refs_1_), channel_id=1, source_target_pairs={{0,4},{4,8},{8,12},{12,0},{1,5},{5,9},{9,13},{13,1},{2,6},{6,10},{... | collective-permute-start | bytes 3538952 | tf_op jit(solution)/shard_map/ppermute | solution.py:144
  143.8 1.0 copy-start.3
  143.8 28.3 %collective-permute-start.3 = (f32[384,768]{1,0:T(8,128)S(1)}, f32[384,768]{1,0:T(8,128)S(1)}, u32[]{:S(2)}, u32[]{:S(2)}) collective-permute-start(f32[384,768]{1,0:T(8,128)S(1)} %collective-permute-done.2.refs_1_), channel_id=1, source_target_pairs={{0,4},{4,8},{8,12},{12,0},{1,5},{5,9},{9,13},{13,1},{2,6},{6,10},{... | collective-permute-start | bytes 3538952 | tf_op jit(solution)/shard_map/ppermute | solution.py:144
  172.2 1.0 copy-start.4
  196.4 4.7 %collective-permute-start.4 = (f32[2,384,768]{2,1,0:T(8,128)S(1)}, f32[2,384,768]{2,1,0:T(8,128)}, u32[]{:S(2)}, u32[]{:S(2)}) collective-permute-start(f32[2,384,768]{2,1,0:T(8,128)S(1)} %dynamic-slice_bitcast_fusion.1), channel_id=1, source_target_pairs={{0,1},{1,0},{2,3},{3,2},{4,5},{5,4},{6,7},{7,6},{8,9},{9,8},{10,11... | collective-permute-start | bytes 7077896 | tf_op jit(solution)/shard_map/ppermute | solution.py:114
  203.8 29.4 %copy-start.2 = (f32[384,768]{1,0:T(8,128)S(1)}, f32[384,768]{1,0:T(8,128)}, u32[]{:S(2)}) copy-start(f32[384,768]{1,0:T(8,128)} %param.4) | copy-start | bytes 3538948
  204.9 28.3 %collective-permute-start.5 = (f32[1,384,768]{2,1,0:T(8,128)}, f32[1,384,768]{2,1,0:T(8,128)}, u32[]{:S(2)}, u32[]{:S(2)}) collective-permute-start(f32[1,384,768]{2,1,0:T(8,128)} %constant_dynamic-slice_fusion.1), channel_id=1, source_target_pairs={{0,2},{1,3},{2,0},{3,1},{4,6},{5,7},{6,4},{7,5},{8,10},{9,11},{10,... | collective-permute-start | bytes 3538952 | tf_op jit(solution)/shard_map/ppermute | solution.py:114
  235.8 1.9 collective-permute-start.6
  237.7 45.3 %copy-start.10 = (f32[384,768]{1,0:T(8,128)}, f32[384,768]{1,0:T(8,128)S(1)}, u32[]{:S(2)}) copy-start(f32[384,768]{1,0:T(8,128)S(1)} %collective-permute-done.6.refs_1_) | copy-start | bytes 3538948
  237.7 66.2 %collective-permute-start.7 = (f32[384,768]{1,0:T(8,128)S(1)}, f32[384,768]{1,0:T(8,128)S(1)}, u32[]{:S(2)}, u32[]{:S(2)}) collective-permute-start(f32[384,768]{1,0:T(8,128)S(1)} %collective-permute-done.6.refs_1_), channel_id=1, source_target_pairs={{0,4},{4,8},{8,12},{12,0},{1,5},{5,9},{9,13},{13,1},{2,6},{6,10},{... | collective-permute-start | bytes 3538952 | tf_op jit(solution)/shard_map/ppermute | solution.py:144
  303.9 36.2 %copy-start.6 = (f32[384,768]{1,0:T(8,128)}, f32[384,768]{1,0:T(8,128)S(1)}, u32[]{:S(2)}) copy-start(f32[384,768]{1,0:T(8,128)S(1)} %collective-permute-done.7.refs_1_) | copy-start | bytes 3538948
  304.0 63.3 %collective-permute-start.8 = (f32[384,768]{1,0:T(8,128)S(1)}, f32[384,768]{1,0:T(8,128)S(1)}, u32[]{:S(2)}, u32[]{:S(2)}) collective-permute-start(f32[384,768]{1,0:T(8,128)S(1)} %collective-permute-done.7.refs_1_), channel_id=1, source_target_pairs={{0,4},{4,8},{8,12},{12,0},{1,5},{5,9},{9,13},{13,1},{2,6},{6,10},{... | collective-permute-start | bytes 3538952 | tf_op jit(solution)/shard_map/ppermute | solution.py:144
  367.3 1.0 copy-start.7
  367.3 28.7 %collective-permute-start.9 = (f32[384,768]{1,0:T(8,128)S(1)}, f32[384,768]{1,0:T(8,128)S(1)}, u32[]{:S(2)}, u32[]{:S(2)}) collective-permute-start(f32[384,768]{1,0:T(8,128)S(1)} %collective-permute-done.8.refs_1_), channel_id=1, source_target_pairs={{0,4},{4,8},{8,12},{12,0},{1,5},{5,9},{9,13},{13,1},{2,6},{6,10},{... | collective-permute-start | bytes 3538952 | tf_op jit(solution)/shard_map/ppermute | solution.py:144
  396.0 1.0 copy-start.8
  418.4 6.6 %copy-start = (f32[1536,768]{1,0:T(8,128)S(1)}, f32[1536,768]{1,0:T(8,128)}, u32[]{:S(2)}) copy-start(f32[1536,768]{1,0:T(8,128)} %shard_map.53) | copy-start | bytes 14155780
  420.3 4.6 collective-permute-start.10
  425.2 28.2 %copy-start.1 = (f32[384,768]{1,0:T(8,128)S(1)}, f32[384,768]{1,0:T(8,128)}, u32[]{:S(2)}) copy-start(f32[384,768]{1,0:T(8,128)} %bitcast_subtract_fusion.1) | copy-start | bytes 3538948
  425.3 28.1 %collective-permute-start.11 = (f32[1,384,768]{2,1,0:T(8,128)S(1)}, f32[1,384,768]{2,1,0:T(8,128)S(1)}, u32[]{:S(2)}, u32[]{:S(2)}) collective-permute-start(f32[1,384,768]{2,1,0:T(8,128)S(1)} %constant_dynamic-slice_fusion), channel_id=1, source_target_pairs={{0,2},{1,3},{2,0},{3,1},{4,6},{5,7},{6,4},{7,5},{8,10},{9,11},{10,... | collective-permute-start | bytes 3538952 | tf_op jit(solution)/shard_map/ppermute | solution.py:114
Sparse Core Ops, SparseCore 0:
  8.9 49.6 all-gather.2
  235.9 47.0 all-gather.4
where the time goes:
time: 470 us; the launch traced here: 462 us
  Pallas kernels  170 us (36%)
  starting transfers between devices  134 us (29%)
  waiting for transfers between devices  127 us (27%)
  between operations  14 us (3%)
  local copies, waits for them, and re-layouts  8.65 us (2%)
  other arithmetic  8.12 us (2%)
    pallas_call x8, Pallas kernels, apply_block(): pl.pallas_call(functools.partial(apply_kernel, times, parts, total is not...  170 us
    ppermute x6, starting transfers between devices, body(): later = [lax.ppermute(p, 'row', ring) for p in piece]  130 us
    ppermute x4, waiting for transfers between devices, scatter_rows(): value = mine + lax.ppermute(theirs, 'col', swap)  65.4 us
    all_gather x2, waiting for transfers between devices, body(): rows = [lax.all_gather(o, 'col', axis=0, tiled=True) for o in own]  37.2 us
    ppermute x6, waiting for transfers between devices, body(): later = [lax.ppermute(p, 'row', ring) for p in piece]  23.5 us
  transfers between devices with their start and end apart: 14, of which 10 were waited for; matrix products, arithmetic and copies ran while one was open for 0% of the time, Pallas kernels for 28%

commit v1 on v0

--- a/solution.py
+++ b/solution.py
@@ -8,6 +8,7 @@
 from jax.sharding import PartitionSpec as P
 
 PASSES = 2
+LANES = 128
 
 
 def split(value):
@@ -97,6 +98,360 @@
     )(*args)
 
 
+def chain_kernel(
+    times, own_ref, weight_ref, screened_ref, out_ref,
+    buf, side, rows, weighted, plain, acc, from_partner, from_twin, tiles,
+    own_sem, row_recv, col_recv, side_recv, partner_recv, twin_recv, tile_sem,
+    partner_send, twin_send, relay_send, down_send, up_send,
+    side_send, cross_send, sum_send, twin_sum_send,
+):
+    n = lax.axis_size("row")
+    r = lax.axis_index("row")
+    c = lax.axis_index("col")
+    x, k = c // 2, c % 2
+    partner, twin, opposite = c + 1 - 2 * k, c + 2 - 4 * x, 3 - c
+    slots, chunk, depth = buf.shape
+    slots = slots // 2
+    pieces = slots // n
+    points = pieces * chunk
+    units = slots // 2
+    diagonal = r == c
+    base = jnp.where(diagonal, 0, slots)
+    end_set = (c == 0) | (c == n - 1)
+    goes_down = (r >= c) & (r < n - 1)
+    goes_up = (r <= c) & (r > 0)
+    relays = (goes_down | goes_up) & jnp.logical_not(diagonal)
+    distance = jnp.where(r > c, r - c, c - r)
+    near = relays & (distance == 1)
+    side_set = (n - 1) * (1 - x)
+    side_next = r + 2 * x - 1
+    side_goes = (side_next >= 0) & (side_next < n)
+    side_source = r == side_set
+
+    def remote(source, target, send, recv, row, col):
+        return pltpu.make_async_remote_copy(
+            src_ref=source, dst_ref=target, send_sem=send, recv_sem=recv,
+            device_id={"row": row, "col": col}, device_id_type=pl.DeviceIdType.MESH,
+        )
+
+    def to_partner(i):
+        q = c * pieces + i
+        return remote(buf.at[q], buf.at[q], partner_send.at[i], row_recv.at[q], r, partner)
+
+    def to_twin(i):
+        q = c * pieces + i
+        return remote(buf.at[q], buf.at[q], twin_send.at[i], row_recv.at[q], r, twin)
+
+    def relay(i):
+        q = twin * pieces + i
+        return remote(buf.at[q], buf.at[q], relay_send.at[i], row_recv.at[q], r, partner)
+
+    def wait_row(col, i):
+        q = col * pieces + i
+        remote(buf.at[q], buf.at[q], partner_send.at[i], row_recv.at[q], r, partner).wait_recv()
+
+    def down(q):
+        return remote(buf.at[base + q], buf.at[slots + q], down_send.at[q], col_recv.at[q], r + 1, c)
+
+    def up(q):
+        return remote(buf.at[base + q], buf.at[slots + q], up_send.at[q], col_recv.at[q], r - 1, c)
+
+    def wait_col(q):
+        remote(buf.at[slots + q], buf.at[slots + q], down_send.at[q], col_recv.at[q], r, partner).wait_recv()
+
+    def forward(q, carried):
+        @pl.when(goes_down & carried)
+        def _():
+            down(q).start()
+
+        @pl.when(goes_up & carried)
+        def _():
+            up(q).start()
+
+    def side_forward(i, source):
+        return remote(source, side.at[i], side_send.at[i], side_recv.at[i], side_next, c)
+
+    def side_cross(i):
+        q = c * pieces + i
+        return remote(side.at[i], buf.at[slots + q], cross_send.at[i], col_recv.at[q], r, side_set)
+
+    def unit_slots(u):
+        half = u // pieces
+        block = 2 * ((x + half) % 2)
+        return block * pieces + u % pieces, (block + 1) * pieces + u % pieces
+
+    def serve(u):
+        carried = jnp.logical_not(end_set) | (u < pieces)
+        for q in unit_slots(u):
+            wait_col(q)
+            forward(q, carried)
+
+    def tile_of(m):
+        return 2 * ((x + 1 + m // 2) % 2) + (k + 1 + m) % 2
+
+    def tile_copies(step):
+        u, m = step // n, step % n
+        slot = step % 2
+        first = pl.multiple_of(tile_of(m) * points, chunk)
+        return [
+            pltpu.make_async_copy(
+                screened_ref.at[:, pl.ds(first, points), pl.ds(pl.multiple_of(q * chunk, chunk), chunk)],
+                tiles.at[slot, :, :, pl.ds(j * chunk, chunk)],
+                tile_sem.at[slot, j],
+            )
+            for j, q in enumerate(unit_slots(u))
+        ]
+
+    def split_rows(col):
+        @pl.loop(0, pieces)
+        def _(i):
+            q = col * pieces + i
+            first = pl.multiple_of(q * chunk, chunk)
+            high, low = split(buf[q])
+            rows[pl.ds(first, chunk), 0:depth] = high
+            rows[pl.ds(first, chunk), depth : 2 * depth] = low
+            rows[pl.ds(first, chunk), 2 * depth : 3 * depth] = high
+
+    def partner_sum(j):
+        block = opposite if j == 0 else partner
+        return remote(acc.at[block], from_partner.at[j], sum_send.at[j], partner_recv.at[j], r, partner)
+
+    def twin_sum(i):
+        part = pl.ds(i * chunk, chunk)
+        return remote(acc.at[twin, part], from_twin.at[part], twin_sum_send.at[i], twin_recv.at[i], r, twin)
+
+    own_copy = pltpu.make_async_copy(own_ref, buf.at[pl.ds(c * pieces, pieces)], own_sem)
+    own_copy.start()
+    for copy in tile_copies(0):
+        copy.start()
+
+    barrier = pltpu.get_barrier_semaphore()
+    for col in (partner, twin, opposite):
+        pl.semaphore_signal(
+            barrier, inc=1, device_id={"row": r, "col": col}, device_id_type=pl.DeviceIdType.MESH
+        )
+
+    @pl.when(r > 0)
+    def _():
+        pl.semaphore_signal(
+            barrier, inc=1, device_id={"row": r - 1, "col": c}, device_id_type=pl.DeviceIdType.MESH
+        )
+
+    @pl.when(r < n - 1)
+    def _():
+        pl.semaphore_signal(
+            barrier, inc=1, device_id={"row": r + 1, "col": c}, device_id_type=pl.DeviceIdType.MESH
+        )
+
+    own_copy.wait()
+    pl.semaphore_wait(barrier, 3 + jnp.where(r > 0, 1, 0) + jnp.where(r < n - 1, 1, 0))
+
+    for i in range(pieces):
+        to_twin(i).start()
+        to_partner(i).start()
+
+        @pl.when(side_source & side_goes)
+        def _():
+            side_forward(i, buf.at[c * pieces + i]).start()
+
+        @pl.when(diagonal)
+        def _():
+            forward(c * pieces + i, True)
+
+    acc[...] = jnp.zeros_like(acc)
+    split_rows(c)
+    for i in range(pieces):
+        wait_row(partner, i)
+
+        @pl.when(diagonal)
+        def _():
+            forward(partner * pieces + i, True)
+
+    split_rows(partner)
+    middle = jnp.logical_not(end_set)
+    for i in range(pieces):
+        wait_row(twin, i)
+        relay(i).start()
+
+        @pl.when(diagonal)
+        def _():
+            forward(twin * pieces + i, middle)
+
+        wait_row(opposite, i)
+
+        @pl.when(diagonal)
+        def _():
+            forward(opposite * pieces + i, middle)
+
+        @pl.when(jnp.logical_not(side_source))
+        def _():
+            pltpu.make_async_remote_copy(
+                src_ref=side.at[i], dst_ref=side.at[i], send_sem=side_send.at[i],
+                recv_sem=side_recv.at[i], device_id={"row": r, "col": partner},
+                device_id_type=pl.DeviceIdType.MESH,
+            ).wait_recv()
+
+            @pl.when(side_goes)
+            def _():
+                side_forward(i, side.at[i]).start()
+
+            side_cross(i).start()
+
+        if i > 0:
+            @pl.when(near)
+            def _():
+                serve(i - 1)
+
+    split_rows(twin)
+    split_rows(opposite)
+
+    @pl.when(relays & jnp.logical_not(near))
+    def _():
+        serve(0)
+
+    ahead = jnp.where(near, 2, 1)
+    steps = units * n
+
+    @pl.loop(0, units)
+    def _(u):
+        @pl.when(jnp.logical_not(diagonal) & jnp.logical_not(relays))
+        def _():
+            for q in unit_slots(u):
+                wait_col(q)
+
+        first, second = unit_slots(u)
+        cols = jnp.concatenate([buf[base + first], buf[base + second]], axis=0)
+        width = cols.shape[0]
+        high, low = split(cols)
+        plain[0:width, :] = high
+        plain[width : 2 * width, :] = high
+        plain[2 * width : 3 * width, :] = low
+        turned = cols.T
+        for t in range(times):
+            high, low = split(turned * weight_ref[:, t : t + 1])
+            weighted[t, 0:depth, :] = high
+            weighted[t, depth : 2 * depth, :] = high
+            weighted[t, 2 * depth : 3 * depth, :] = low
+
+        @pl.loop(0, n)
+        def _(m):
+            step = u * n + m
+
+            @pl.when((m == n // 2) & relays & (u + ahead < units))
+            def _():
+                serve(u + ahead)
+
+            @pl.when(step + 1 < steps)
+            def _():
+                for copy in tile_copies(step + 1):
+                    copy.start()
+
+            for copy in tile_copies(step):
+                copy.wait()
+            tile = tile_of(m)
+            left = rows[pl.ds(pl.multiple_of(tile * points, chunk), points), :]
+            mixed = None
+            for t in range(times):
+                green = jnp.dot(left, weighted[t], preferred_element_type=jnp.float32)
+                term = green * tiles[step % 2, t]
+                mixed = term if mixed is None else mixed + term
+            high, low = split(mixed)
+            mixed = jnp.concatenate([high, low, high], axis=1)
+            acc[tile] = acc[tile] + jnp.dot(mixed, plain[...], preferred_element_type=jnp.float32)
+
+            @pl.when((u == units - 1) & (m == 0))
+            def _():
+                partner_sum(0).start()
+
+            @pl.when((u == units - 1) & (m == 1))
+            def _():
+                partner_sum(0).wait_recv()
+                for i in range(pieces):
+                    part = slice(i * chunk, (i + 1) * chunk)
+                    acc[twin, part, :] = acc[twin, part, :] + from_partner[0, part, :]
+                    twin_sum(i).start()
+
+            @pl.when((u == units - 1) & (m == 2))
+            def _():
+                partner_sum(1).start()
+
+    partner_sum(1).wait_recv()
+    for i in range(pieces):
+        part = slice(i * chunk, (i + 1) * chunk)
+        mine = acc[c, part, :] + from_partner[1, part, :]
+        twin_sum(i).wait_recv()
+        out_ref[part, :] = buf[c * pieces + i] - (mine + from_twin[part, :])
+
+    for i in range(pieces):
+        to_twin(i).wait_send()
+        to_partner(i).wait_send()
+        relay(i).wait_send()
+        twin_sum(i).wait_send()
+
+        @pl.when(side_goes)
+        def _():
+            side_forward(i, side.at[i]).wait_send()
+
+        @pl.when(jnp.logical_not(side_source))
+        def _():
+            side_cross(i).wait_send()
+
+    for j in range(2):
+        partner_sum(j).wait_send()
+    for q in range(slots):
+        carried = middle | (x == q // (2 * pieces))
+
+        @pl.when(goes_down & carried)
+        def _():
+            down(q).wait_send()
+
+        @pl.when(goes_up & carried)
+        def _():
+            up(q).wait_send()
+
+
+def chain_pass(step, orbitals, weight, screened):
+    times, n_rows, n_cols = screened.shape
+    points, depth = orbitals.shape
+    n = n_rows // points
+    pieces = 3
+    chunk = points // pieces
+    slots = n * pieces
+    dma = pltpu.SemaphoreType.DMA
+    return pl.pallas_call(
+        functools.partial(chain_kernel, times),
+        out_shape=jax.ShapeDtypeStruct((points, depth), jnp.float32),
+        in_specs=[
+            pl.BlockSpec(memory_space=pl.ANY),
+            pl.BlockSpec(memory_space=pltpu.VMEM),
+            pl.BlockSpec(memory_space=pl.ANY),
+        ],
+        out_specs=pl.BlockSpec(memory_space=pltpu.VMEM),
+        scratch_shapes=[
+            pltpu.VMEM((2 * slots, chunk, depth), jnp.float32),
+            pltpu.VMEM((pieces, chunk, depth), jnp.float32),
+            pltpu.VMEM((n_rows, 3 * depth), jnp.bfloat16),
+            pltpu.VMEM((times, 3 * depth, 2 * chunk), jnp.bfloat16),
+            pltpu.VMEM((6 * chunk, depth), jnp.bfloat16),
+            pltpu.VMEM((n, points, depth), jnp.float32),
+            pltpu.VMEM((2, points, depth), jnp.float32),
+            pltpu.VMEM((points, depth), jnp.float32),
+            pltpu.VMEM((2, times, points, 2 * chunk), jnp.float32),
+            dma(()), dma((slots,)), dma((slots,)), dma((pieces,)), dma((2,)), dma((pieces,)), dma((2, 2)),
+            dma((pieces,)), dma((pieces,)), dma((pieces,)), dma((slots,)), dma((slots,)),
+            dma((pieces,)), dma((pieces,)), dma((2,)), dma((pieces,)),
+        ],
+        compiler_params=pltpu.CompilerParams(
+            collective_id=step, has_side_effects=True, vmem_limit_bytes=60 * 1024 * 1024
+        ),
+        cost_estimate=pl.CostEstimate(
+            flops=6 * (times + 1) * n_rows * n_cols * depth,
+            bytes_accessed=4 * times * n_rows * n_cols,
+            transcendentals=0,
+        ),
+    )(orbitals.reshape(pieces, chunk, depth), weight.T, screened)
+
+
 def scatter_rows(value):
     n_col = lax.axis_size("col")
     if n_col & (n_col - 1):
@@ -122,6 +477,10 @@
     factor = n_col // n_row
     points, depth = orbitals.shape
     weight = green_weight * time_weight[:, None]
+    if n_row == 4 and n_col == 4 and points % 3 == 0 and (points // 3) % LANES == 0:
+        for step in range(PASSES):
+            orbitals = chain_pass(step, orbitals, weight, screened)
+        return orbitals
     to_columns = [
         ((c // factor) * n_col + (c % factor) * n_row + m, m * n_col + c)
         for m in range(n_row)

time: 470 us -> 363 us (0.77); the launches traced: 462 us -> 362 us
  Pallas kernels: 170 us -> 358 us
  starting transfers between devices: 134 us -> 0 us
  waiting for transfers between devices: 127 us -> 0 us
  between operations: 14 us -> 0.02 us
  other arithmetic: 8.12 us -> 0.78 us
  local copies, waits for them, and re-layouts: 8.65 us -> 3.3 us
    pallas_call x8 -> x2, Pallas kernels: 170 us -> 358 us  [chain_pass(): pl.pallas_call(functools.partial(chain_kernel, times), out_shape=jax.Shap...]
    ppermute x12 -> x0, starting transfers between devices: 134 us -> none  [the longest x6 130 us: body(): later = [lax.ppermute(p, 'row', ring) for p in piece]]
    ppermute x12 -> x0, waiting for transfers between devices: 88.9 us -> none  [the longest x4 65.4 us: scatter_rows(): value = mine + lax.ppermute(theirs, 'col', swap)]
    all_gather x2 -> x0, waiting for transfers between devices: 37.2 us -> none  [body(): rows = [lax.all_gather(o, 'col', axis=0, tiled=True) for o in own]]
    squeeze x4 -> x0, local copies, waits for them, and re-layouts: 4.97 us -> none  [scatter_rows(): theirs = lax.dynamic_index_in_dim(pairs, 1 - bit, 1, keepdims=False)]
  transfers between devices with their start and end apart: 14 -> 0, of which waited for: 10 -> 0; matrix products, arithmetic and copies ran while one was open for 0% -> 0% of each run, Pallas kernels for 28% -> 0%
where the time goes in v1:
time: 363 us; the launch traced here: 362 us
  Pallas kernels  358 us (99%)
    pallas_call x2, Pallas kernels, chain_pass(): pl.pallas_call(functools.partial(chain_kernel, times), out_shape=jax.Shap...  358 us

profile of v1, /device:TPU:0, one launch (start us, length us, event | category | flops | bytes accessed | tf_op | source)
XLA Modules:
  0.0 361.8 jit_solution(1301569626091027872)
XLA Ops:
  0.0 0.8 broadcast_multiply_fusion
  0.8 0.9 copy.7
  1.7 180.2 %shard_map.46 = f32[384,768]{1,0:T(8,128)} custom-call(f32[3,128,768]{2,1,0:T(8,128)} %bitcast.5, f32[768,3]{1,0:T(8,128)} %bitcast.3, f32[3,1536,1536]{2,1,0:T(8,128)} %screened_ref.3), custom_call_target="tpu_custom_call" | custom-call | flops 43486543872 | bytes 28311552 | tf_op jit(solution)/shard_map/pallas_call | solution.py:421
  182.0 177.4 %shard_map.47 = f32[384,768]{1,0:T(8,128)} custom-call(f32[3,128,768]{2,1,0:T(8,128)} %bitcast.6, f32[768,3]{1,0:T(8,128)} %bitcast.4, f32[3,1536,1536]{2,1,0:T(8,128)} %screened_ref.3), custom_call_target="tpu_custom_call" | custom-call | flops 43486543872 | bytes 28311552 | tf_op jit(solution)/shard_map/pallas_call | solution.py:421
  359.4 2.4 copy.9

commit v2 on v1

--- a/solution.py
+++ b/solution.py
@@ -100,33 +100,29 @@
 
 def chain_kernel(
     times, own_ref, weight_ref, screened_ref, out_ref,
-    buf, side, rows, weighted, plain, acc, from_partner, from_twin, tiles,
+    buf, rows, weighted, plain, acc, from_partner, from_twin, tiles,
     own_sem, row_recv, col_recv, side_recv, partner_recv, twin_recv, tile_sem,
     partner_send, twin_send, relay_send, down_send, up_send,
-    side_send, cross_send, sum_send, twin_sum_send,
+    side_down_send, side_up_send, cross_send, sum_send, twin_sum_send,
 ):
     n = lax.axis_size("row")
     r = lax.axis_index("row")
     c = lax.axis_index("col")
     x, k = c // 2, c % 2
     partner, twin, opposite = c + 1 - 2 * k, c + 2 - 4 * x, 3 - c
-    slots, chunk, depth = buf.shape
-    slots = slots // 2
-    pieces = slots // n
+    pieces, chunk, depth = own_ref.shape
+    slots = n * pieces
     points = pieces * chunk
     units = slots // 2
+    half_units = units // 2
     diagonal = r == c
     base = jnp.where(diagonal, 0, slots)
-    end_set = (c == 0) | (c == n - 1)
     goes_down = (r >= c) & (r < n - 1)
     goes_up = (r <= c) & (r > 0)
     relays = (goes_down | goes_up) & jnp.logical_not(diagonal)
     distance = jnp.where(r > c, r - c, c - r)
     near = relays & (distance == 1)
-    side_set = (n - 1) * (1 - x)
-    side_next = r + 2 * x - 1
-    side_goes = (side_next >= 0) & (side_next < n)
-    side_source = r == side_set
+    far = relays & jnp.logical_not(near)
 
     def remote(source, target, send, recv, row, col):
         return pltpu.make_async_remote_copy(
@@ -159,38 +155,87 @@
     def wait_col(q):
         remote(buf.at[slots + q], buf.at[slots + q], down_send.at[q], col_recv.at[q], r, partner).wait_recv()
 
-    def forward(q, carried):
-        @pl.when(goes_down & carried)
+    def forward(q):
+        @pl.when(goes_down)
         def _():
             down(q).start()
 
-        @pl.when(goes_up & carried)
+        @pl.when(goes_up)
         def _():
             up(q).start()
 
-    def side_forward(i, source):
-        return remote(source, side.at[i], side_send.at[i], side_recv.at[i], side_next, c)
-
-    def side_cross(i):
+    side_count = pieces - 1
+
+    def side_set(e):
+        return 2 * (1 - x) + e
+
+    def side_goes_down(e):
+        return (r >= side_set(e)) & (r < n - 1)
+
+    def side_goes_up(e):
+        return (r <= side_set(e)) & (r > 0)
+
+    def side_source(e, i):
+        own = c * pieces + i
+        place = 2 * slots + e * side_count + i - 1
+        return buf.at[jnp.where(r == side_set(e), own, place)]
+
+    def side_down(e, i):
+        j = e * side_count + i - 1
+        return remote(side_source(e, i), buf.at[2 * slots + j], side_down_send.at[j], side_recv.at[j], r + 1, c)
+
+    def side_up(e, i):
+        j = e * side_count + i - 1
+        return remote(side_source(e, i), buf.at[2 * slots + j], side_up_send.at[j], side_recv.at[j], r - 1, c)
+
+    def side_cross(e, i):
+        j = e * side_count + i - 1
         q = c * pieces + i
-        return remote(side.at[i], buf.at[slots + q], cross_send.at[i], col_recv.at[q], r, side_set)
+        return remote(buf.at[2 * slots + j], buf.at[slots + q], cross_send.at[j], col_recv.at[q], r, side_set(e))
+
+    def side_forward(e, i):
+        @pl.when(side_goes_down(e))
+        def _():
+            side_down(e, i).start()
+
+        @pl.when(side_goes_up(e))
+        def _():
+            side_up(e, i).start()
+
+    def side_serve(i):
+        for e in range(2):
+            @pl.when(r != side_set(e))
+            def _():
+                j = e * side_count + i - 1
+                here = buf.at[2 * slots + j]
+                remote(here, here, cross_send.at[j], side_recv.at[j], r, partner).wait_recv()
+                side_forward(e, i)
+                side_cross(e, i).start()
 
     def unit_slots(u):
-        half = u // pieces
+        half = jnp.where((u == 2) | (u >= 4), 1, 0)
+        piece = ((u + 1) // 2) % pieces
         block = 2 * ((x + half) % 2)
-        return block * pieces + u % pieces, (block + 1) * pieces + u % pieces
+        return block * pieces + piece, (block + 1) * pieces + piece
 
     def serve(u):
-        carried = jnp.logical_not(end_set) | (u < pieces)
         for q in unit_slots(u):
             wait_col(q)
-            forward(q, carried)
+            forward(q)
+
+    def place_of(step):
+        whole = half_units * n
+        late = step - whole
+        second = jnp.where(late < units, late, late - units)
+        u = jnp.where(step < whole, step // n, half_units + second // 2)
+        m = jnp.where(step < whole, step % n, second % 2 + jnp.where(late < units, 0, 2))
+        return u, m
 
     def tile_of(m):
         return 2 * ((x + 1 + m // 2) % 2) + (k + 1 + m) % 2
 
     def tile_copies(step):
-        u, m = step // n, step % n
+        u, m = place_of(step)
         slot = step % 2
         first = pl.multiple_of(tile_of(m) * points, chunk)
         return [
@@ -250,130 +295,121 @@
         to_twin(i).start()
         to_partner(i).start()
 
-        @pl.when(side_source & side_goes)
-        def _():
-            side_forward(i, buf.at[c * pieces + i]).start()
-
         @pl.when(diagonal)
         def _():
-            forward(c * pieces + i, True)
+            forward(c * pieces + i)
+
+    for i in range(1, pieces):
+        for e in range(2):
+            @pl.when(r == side_set(e))
+            def _():
+                side_forward(e, i)
 
     acc[...] = jnp.zeros_like(acc)
-    split_rows(c)
     for i in range(pieces):
         wait_row(partner, i)
 
         @pl.when(diagonal)
         def _():
-            forward(partner * pieces + i, True)
-
+            forward(partner * pieces + i)
+
+    split_rows(c)
     split_rows(partner)
-    middle = jnp.logical_not(end_set)
     for i in range(pieces):
-        wait_row(twin, i)
-        relay(i).start()
-
-        @pl.when(diagonal)
-        def _():
-            forward(twin * pieces + i, middle)
-
-        wait_row(opposite, i)
-
-        @pl.when(diagonal)
-        def _():
-            forward(opposite * pieces + i, middle)
-
-        @pl.when(jnp.logical_not(side_source))
-        def _():
-            pltpu.make_async_remote_copy(
-                src_ref=side.at[i], dst_ref=side.at[i], send_sem=side_send.at[i],
-                recv_sem=side_recv.at[i], device_id={"row": r, "col": partner},
-                device_id_type=pl.DeviceIdType.MESH,
-            ).wait_recv()
-
-            @pl.when(side_goes)
-            def _():
-                side_forward(i, side.at[i]).start()
-
-            side_cross(i).start()
+        for col in (twin, opposite):
+            wait_row(col, i)
+            if col is twin:
+                relay(i).start()
+            if i == 0:
+                @pl.when(diagonal)
+                def _():
+                    forward(col * pieces + i)
 
         if i > 0:
             @pl.when(near)
             def _():
                 serve(i - 1)
 
+    side_serve(1)
     split_rows(twin)
     split_rows(opposite)
 
-    @pl.when(relays & jnp.logical_not(near))
+    @pl.when(far)
     def _():
         serve(0)
 
-    ahead = jnp.where(near, 2, 1)
     steps = units * n
-
-    @pl.loop(0, units)
-    def _(u):
-        @pl.when(jnp.logical_not(diagonal) & jnp.logical_not(relays))
-        def _():
-            for q in unit_slots(u):
-                wait_col(q)
-
-        first, second = unit_slots(u)
-        cols = jnp.concatenate([buf[base + first], buf[base + second]], axis=0)
-        width = cols.shape[0]
-        high, low = split(cols)
-        plain[0:width, :] = high
-        plain[width : 2 * width, :] = high
-        plain[2 * width : 3 * width, :] = low
-        turned = cols.T
+    whole = half_units * n
+
+    @pl.loop(0, steps)
+    def _(step):
+        u, m = place_of(step)
+        keep = jnp.where(u < half_units, 0, u - half_units)
+
+        for unit, near_step, far_step in ((1, steps, 4), (3, 5, 9), (5, 10, 15)):
+            @pl.when(relays & (step == jnp.where(near, near_step, far_step)))
+            def _():
+                serve(unit)
+
+        @pl.when(step == n)
+        def _():
+            side_serve(2)
+
+        @pl.when(step + 1 < steps)
+        def _():
+            for copy in tile_copies(step + 1):
+                copy.start()
+
+        @pl.when((m == 0) & (step < whole + units))
+        def _():
+            first, second = unit_slots(u)
+
+            @pl.when(jnp.logical_not(diagonal) & (jnp.logical_not(relays) | (u == 2) | (u == 4)))
+            def _():
+                wait_col(first)
+                wait_col(second)
+
+            cols = jnp.concatenate([buf[base + first], buf[base + second]], axis=0)
+            width = cols.shape[0]
+            high, low = split(cols)
+            plain[keep, 0:width, :] = high
+            plain[keep, width : 2 * width, :] = high
+            plain[keep, 2 * width : 3 * width, :] = low
+            turned = cols.T
+            for t in range(times):
+                high, low = split(turned * weight_ref[:, t : t + 1])
+                weighted[keep, t, 0:depth, :] = high
+                weighted[keep, t, depth : 2 * depth, :] = high
+                weighted[keep, t, 2 * depth : 3 * depth, :] = low
+
+        for copy in tile_copies(step):
+            copy.wait()
+        tile = tile_of(m)
+        left = rows[pl.ds(pl.multiple_of(tile * points, chunk), points), :]
+        mixed = None
         for t in range(times):
-            high, low = split(turned * weight_ref[:, t : t + 1])
-            weighted[t, 0:depth, :] = high
-            weighted[t, depth : 2 * depth, :] = high
-            weighted[t, 2 * depth : 3 * depth, :] = low
-
-        @pl.loop(0, n)
-        def _(m):
-            step = u * n + m
-
-            @pl.when((m == n // 2) & relays & (u + ahead < units))
-            def _():
-                serve(u + ahead)
-
-            @pl.when(step + 1 < steps)
-            def _():
-                for copy in tile_copies(step + 1):
-                    copy.start()
-
-            for copy in tile_copies(step):
-                copy.wait()
-            tile = tile_of(m)
-            left = rows[pl.ds(pl.multiple_of(tile * points, chunk), points), :]
-            mixed = None
-            for t in range(times):
-                green = jnp.dot(left, weighted[t], preferred_element_type=jnp.float32)
-                term = green * tiles[step % 2, t]
-                mixed = term if mixed is None else mixed + term
-            high, low = split(mixed)
-            mixed = jnp.concatenate([high, low, high], axis=1)
-            acc[tile] = acc[tile] + jnp.dot(mixed, plain[...], preferred_element_type=jnp.float32)
-
-            @pl.when((u == units - 1) & (m == 0))
-            def _():
-                partner_sum(0).start()
-
-            @pl.when((u == units - 1) & (m == 1))
-            def _():
-                partner_sum(0).wait_recv()
-                for i in range(pieces):
-                    part = slice(i * chunk, (i + 1) * chunk)
-                    acc[twin, part, :] = acc[twin, part, :] + from_partner[0, part, :]
-                    twin_sum(i).start()
-
-            @pl.when((u == units - 1) & (m == 2))
-            def _():
-                partner_sum(1).start()
+            green = jnp.dot(left, weighted[keep, t], preferred_element_type=jnp.float32)
+            term = green * tiles[step % 2, t]
+            mixed = term if mixed is None else mixed + term
+        high, low = split(mixed)
+        mixed = jnp.concatenate([high, low, high], axis=1)
+        acc[tile] = acc[tile] + jnp.dot(mixed, plain[keep], preferred_element_type=jnp.float32)
+
+        @pl.when((u == units - 1) & (m == 0))
+        def _():
+            partner_sum(0).start()
+
+        @pl.when((u == units - 1) & (m == 1))
+        def _():
+            partner_sum(0).wait_recv()
+            for i in range(pieces):
+                part = slice(i * chunk, (i + 1) * chunk)
+                acc[twin, part, :] = acc[twin, part, :] + from_partner[0, part, :]
+                twin_sum(i).start()
+
+        @pl.when((u == units - 1) & (m == 2))
+        def _():
+            partner_sum(1).start()
 
     partner_sum(1).wait_recv()
     for i in range(pieces):
@@ -388,26 +424,31 @@
         relay(i).wait_send()
         twin_sum(i).wait_send()
 
-        @pl.when(side_goes)
-        def _():
-            side_forward(i, side.at[i]).wait_send()
-
-        @pl.when(jnp.logical_not(side_source))
-        def _():
-            side_cross(i).wait_send()
+    for i in range(1, pieces):
+        for e in range(2):
+            @pl.when(side_goes_down(e))
+            def _():
+                side_down(e, i).wait_send()
+
+            @pl.when(side_goes_up(e))
+            def _():
+                side_up(e, i).wait_send()
+
+            @pl.when(r != side_set(e))
+            def _():
+                side_cross(e, i).wait_send()
 
     for j in range(2):
         partner_sum(j).wait_send()
-    for q in range(slots):
-        carried = middle | (x == q // (2 * pieces))
-
-        @pl.when(goes_down & carried)
-        def _():
-            down(q).wait_send()
-
-        @pl.when(goes_up & carried)
-        def _():
-            up(q).wait_send()
+    for u in (0, 1, 3, 5):
+        for q in unit_slots(u):
+            @pl.when(goes_down)
+            def _():
+                down(q).wait_send()
+
+            @pl.when(goes_up)
+            def _():
+                up(q).wait_send()
 
 
 def chain_pass(step, orbitals, weight, screened):
@@ -428,18 +469,17 @@
         ],
         out_specs=pl.BlockSpec(memory_space=pltpu.VMEM),
         scratch_shapes=[
-            pltpu.VMEM((2 * slots, chunk, depth), jnp.float32),
-            pltpu.VMEM((pieces, chunk, depth), jnp.float32),
+            pltpu.VMEM((2 * slots + 2 * (pieces - 1), chunk, depth), jnp.float32),
             pltpu.VMEM((n_rows, 3 * depth), jnp.bfloat16),
-            pltpu.VMEM((times, 3 * depth, 2 * chunk), jnp.bfloat16),
-            pltpu.VMEM((6 * chunk, depth), jnp.bfloat16),
+            pltpu.VMEM((pieces, times, 3 * depth, 2 * chunk), jnp.bfloat16),
+            pltpu.VMEM((pieces, 6 * chunk, depth), jnp.bfloat16),
             pltpu.VMEM((n, points, depth), jnp.float32),
             pltpu.VMEM((2, points, depth), jnp.float32),
             pltpu.VMEM((points, depth), jnp.float32),
             pltpu.VMEM((2, times, points, 2 * chunk), jnp.float32),
-            dma(()), dma((slots,)), dma((slots,)), dma((pieces,)), dma((2,)), dma((pieces,)), dma((2, 2)),
+            dma(()), dma((slots,)), dma((slots,)), dma((2 * (pieces - 1),)), dma((2,)), dma((pieces,)), dma((2, 2)),
             dma((pieces,)), dma((pieces,)), dma((pieces,)), dma((slots,)), dma((slots,)),
-            dma((pieces,)), dma((pieces,)), dma((2,)), dma((pieces,)),
+            dma((2 * (pieces - 1),)), dma((2 * (pieces - 1),)), dma((2 * (pieces - 1),)), dma((2,)), dma((pieces,)),
         ],
         compiler_params=pltpu.CompilerParams(
             collective_id=step, has_side_effects=True, vmem_limit_bytes=60 * 1024 * 1024

time: 363 us -> 306 us (0.84)
  Pallas kernels: 358 us -> 301 us
    pallas_call x2, Pallas kernels: 358 us -> 301 us  [chain_pass(): pl.pallas_call(functools.partial(chain_kernel, times), out_shape=jax.Shap...]
where the time goes in v2:
time: 306 us; the launch traced here: 305 us
  Pallas kernels  301 us (98%)
  local copies, waits for them, and re-layouts  3.3 us (1%)
    pallas_call x2, Pallas kernels, chain_pass(): pl.pallas_call(functools.partial(chain_kernel, times), out_shape=jax.Shap...  301 us

profile of v2, /device:TPU:0, one launch (start us, length us, event | category | flops | bytes accessed | tf_op | source)
XLA Modules:
  0.0 305.2 jit_solution(14060659318110700725)
XLA Ops:
  0.0 0.8 broadcast_multiply_fusion
  0.8 0.9 copy.7
  1.7 150.8 %shard_map.46 = f32[384,768]{1,0:T(8,128)} custom-call(f32[3,128,768]{2,1,0:T(8,128)} %bitcast.5, f32[768,3]{1,0:T(8,128)} %bitcast.3, f32[3,1536,1536]{2,1,0:T(8,128)} %screened_ref.3), custom_call_target="tpu_custom_call" | custom-call | flops 43486543872 | bytes 28311552 | tf_op jit(solution)/shard_map/pallas_call | solution.py:462
  152.5 150.3 %shard_map.47 = f32[384,768]{1,0:T(8,128)} custom-call(f32[3,128,768]{2,1,0:T(8,128)} %bitcast.6, f32[768,3]{1,0:T(8,128)} %bitcast.4, f32[3,1536,1536]{2,1,0:T(8,128)} %screened_ref.3), custom_call_target="tpu_custom_call" | custom-call | flops 43486543872 | bytes 28311552 | tf_op jit(solution)/shard_map/pallas_call | solution.py:462
  302.9 2.4 copy.9

commit v3 on v0

--- a/solution.py
+++ b/solution.py
@@ -1,4 +1,5 @@
 import functools
+import types
 
 import jax
 import jax.numpy as jnp
@@ -8,6 +9,7 @@
 from jax.sharding import PartitionSpec as P
 
 PASSES = 2
+LANES = 128
 
 
 def split(value):
@@ -97,6 +99,428 @@
     )(*args)
 
 
+def chain_kernel(
+    passes, times, own_ref, weight_ref, screened_ref, out_ref,
+    buf, rows, weighted, plain, acc, from_partner, from_twin, tiles, turned_weight,
+    own_sem, row_recv, col_recv, side_recv, partner_recv, twin_recv, tile_sem,
+    partner_send, twin_send, relay_send, down_send, up_send,
+    side_down_send, side_up_send, cross_send, sum_send, twin_sum_send,
+):
+    n = lax.axis_size("row")
+    r = lax.axis_index("row")
+    c = lax.axis_index("col")
+    x, k = c // 2, c % 2
+    partner, twin, opposite = c + 1 - 2 * k, c + 2 - 4 * x, 3 - c
+    pieces, chunk, depth = own_ref.shape
+    slots = n * pieces
+    points = pieces * chunk
+    units = slots // 2
+    half_units = units // 2
+    diagonal = r == c
+    base = jnp.where(diagonal, 0, slots)
+    goes_down = (r >= c) & (r < n - 1)
+    goes_up = (r <= c) & (r > 0)
+    relays = (goes_down | goes_up) & jnp.logical_not(diagonal)
+    distance = jnp.where(r > c, r - c, c - r)
+    near = relays & (distance == 1)
+    far = relays & jnp.logical_not(near)
+
+    stride = 2 * slots + 2 * (pieces - 1)
+    side_count = pieces - 1
+    steps = units * n
+    whole = half_units * n
+
+    def remote(source, target, send, recv, row, col):
+        return pltpu.make_async_remote_copy(
+            src_ref=source, dst_ref=target, send_sem=send, recv_sem=recv,
+            device_id={"row": row, "col": col}, device_id_type=pl.DeviceIdType.MESH,
+        )
+
+    def side_set(e):
+        return 2 * (1 - x) + e
+
+    def side_goes_down(e):
+        return (r >= side_set(e)) & (r < n - 1)
+
+    def side_goes_up(e):
+        return (r <= side_set(e)) & (r > 0)
+
+    def unit_slots(u):
+        half = jnp.where((u == 2) | (u >= 4), 1, 0)
+        piece = ((u + 1) // 2) % pieces
+        block = 2 * ((x + half) % 2)
+        return block * pieces + piece, (block + 1) * pieces + piece
+
+    def place_of(step):
+        late = step - whole
+        second = jnp.where(late < units, late, late - units)
+        u = jnp.where(step < whole, step // n, half_units + second // 2)
+        m = jnp.where(step < whole, step % n, second % 2 + jnp.where(late < units, 0, 2))
+        return u, m
+
+    def tile_of(m):
+        return 2 * ((x + 1 + m // 2) % 2) + (k + 1 + m) % 2
+
+    def tile_copies(step):
+        u, m = place_of(step)
+        slot = step % 2
+        first = pl.multiple_of(tile_of(m) * points, chunk)
+        return [
+            pltpu.make_async_copy(
+                screened_ref.at[:, pl.ds(first, points), pl.ds(pl.multiple_of(q * chunk, chunk), chunk)],
+                tiles.at[slot, :, :, pl.ds(j * chunk, chunk)],
+                tile_sem.at[slot, j],
+            )
+            for j, q in enumerate(unit_slots(u))
+        ]
+
+    def moves(p):
+        at = p * stride
+
+        def to_partner(i):
+            q = c * pieces + i
+            return remote(buf.at[at + q], buf.at[at + q], partner_send.at[i], row_recv.at[p * slots + q], r, partner)
+
+        def to_twin(i):
+            q = c * pieces + i
+            return remote(buf.at[at + q], buf.at[at + q], twin_send.at[i], row_recv.at[p * slots + q], r, twin)
+
+        def relay(i):
+            q = twin * pieces + i
+            return remote(buf.at[at + q], buf.at[at + q], relay_send.at[i], row_recv.at[p * slots + q], r, partner)
+
+        def wait_row(col, i):
+            q = col * pieces + i
+            remote(buf.at[at + q], buf.at[at + q], partner_send.at[i], row_recv.at[p * slots + q], r, partner).wait_recv()
+
+        def down(q):
+            return remote(buf.at[at + base + q], buf.at[at + slots + q], down_send.at[q], col_recv.at[p * slots + q], r + 1, c)
+
+        def up(q):
+            return remote(buf.at[at + base + q], buf.at[at + slots + q], up_send.at[q], col_recv.at[p * slots + q], r - 1, c)
+
+        def wait_col(q):
+            remote(buf.at[at + slots + q], buf.at[at + slots + q], down_send.at[q], col_recv.at[p * slots + q], r, partner).wait_recv()
+
+        def forward(q):
+            @pl.when(goes_down)
+            def _():
+                down(q).start()
+
+            @pl.when(goes_up)
+            def _():
+                up(q).start()
+
+        def side_source(e, i):
+            own = c * pieces + i
+            place = 2 * slots + e * side_count + i - 1
+            return buf.at[at + jnp.where(r == side_set(e), own, place)]
+
+        def side_down(e, i):
+            j = e * side_count + i - 1
+            return remote(side_source(e, i), buf.at[at + 2 * slots + j], side_down_send.at[j], side_recv.at[p * 2 * side_count + j], r + 1, c)
+
+        def side_up(e, i):
+            j = e * side_count + i - 1
+            return remote(side_source(e, i), buf.at[at + 2 * slots + j], side_up_send.at[j], side_recv.at[p * 2 * side_count + j], r - 1, c)
+
+        def side_cross(e, i):
+            j = e * side_count + i - 1
+            q = c * pieces + i
+            return remote(buf.at[at + 2 * slots + j], buf.at[at + slots + q], cross_send.at[j], col_recv.at[p * slots + q], r, side_set(e))
+
+        def side_forward(e, i):
+            @pl.when(side_goes_down(e))
+            def _():
+                side_down(e, i).start()
+
+            @pl.when(side_goes_up(e))
+            def _():
+                side_up(e, i).start()
+
+        def side_serve(i):
+            for e in range(2):
+                @pl.when(r != side_set(e))
+                def _():
+                    j = e * side_count + i - 1
+                    here = buf.at[at + 2 * slots + j]
+                    remote(here, here, cross_send.at[j], side_recv.at[p * 2 * side_count + j], r, partner).wait_recv()
+                    side_forward(e, i)
+                    side_cross(e, i).start()
+
+        def serve(u):
+            for q in unit_slots(u):
+                wait_col(q)
+                forward(q)
+
+        def split_rows(col):
+            @pl.loop(0, pieces)
+            def _(i):
+                q = col * pieces + i
+                first = pl.multiple_of(q * chunk, chunk)
+                high, low = split(buf[at + q])
+                rows[pl.ds(first, chunk), 0:depth] = high
+                rows[pl.ds(first, chunk), depth : 2 * depth] = low
+
+        def partner_sum(j):
+            block = opposite if j == 0 else partner
+            return remote(acc.at[block], from_partner.at[2 * p + j], sum_send.at[j], partner_recv.at[2 * p + j], r, partner)
+
+        def twin_sum(i):
+            part = pl.ds(i * chunk, chunk)
+            return remote(acc.at[twin, part], from_twin.at[p, part], twin_sum_send.at[i], twin_recv.at[p * pieces + i], r, twin)
+
+        def launch(i):
+            to_twin(i).start()
+            to_partner(i).start()
+
+            @pl.when(diagonal)
+            def _():
+                forward(c * pieces + i)
+
+            if i > 0:
+                for e in range(2):
+                    @pl.when(r == side_set(e))
+                    def _():
+                        side_forward(e, i)
+
+        return types.SimpleNamespace(**locals())
+
+    own_copy = pltpu.make_async_copy(own_ref, buf.at[pl.ds(c * pieces, pieces)], own_sem)
+    own_copy.start()
+    barrier = pltpu.get_barrier_semaphore()
+    for col in (partner, twin, opposite):
+        pl.semaphore_signal(
+            barrier, inc=1, device_id={"row": r, "col": col}, device_id_type=pl.DeviceIdType.MESH
+        )
+
+    @pl.when(r > 0)
+    def _():
+        pl.semaphore_signal(
+            barrier, inc=1, device_id={"row": r - 1, "col": c}, device_id_type=pl.DeviceIdType.MESH
+        )
+
+    @pl.when(r < n - 1)
+    def _():
+        pl.semaphore_signal(
+            barrier, inc=1, device_id={"row": r + 1, "col": c}, device_id_type=pl.DeviceIdType.MESH
+        )
+
+    own_copy.wait()
+    pl.semaphore_wait(barrier, 3 + jnp.where(r > 0, 1, 0) + jnp.where(r < n - 1, 1, 0))
+
+    turned_weight[...] = weight_ref[...].T
+    acc[...] = jnp.zeros_like(acc)
+    first_pass = moves(0)
+    for i in range(pieces):
+        first_pass.launch(i)
+
+    @pl.loop(0, passes)
+    def _(p):
+        v = moves(p)
+        for copy in tile_copies(0):
+            copy.start()
+
+        for i in range(pieces):
+            v.wait_row(partner, i)
+
+            @pl.when(diagonal)
+            def _():
+                v.forward(partner * pieces + i)
+
+        v.split_rows(c)
+        v.split_rows(partner)
+        for i in range(pieces):
+            for col in (twin, opposite):
+                v.wait_row(col, i)
+                if col is twin:
+                    v.relay(i).start()
+                if i == 0:
+                    @pl.when(diagonal)
+                    def _():
+                        v.forward(col * pieces + i)
+
+            if i > 0:
+                @pl.when(near)
+                def _():
+                    v.serve(i - 1)
+
+        v.side_serve(1)
+        v.split_rows(twin)
+        v.split_rows(opposite)
+
+        @pl.when(far)
+        def _():
+            v.serve(0)
+
+        @pl.loop(0, steps)
+        def _(step):
+            u, m = place_of(step)
+            keep = jnp.where(u < half_units, 0, u - half_units)
+
+            for unit, near_step, far_step in ((1, steps, 4), (3, 5, 9), (5, 10, 15)):
+                @pl.when(relays & (step == jnp.where(near, near_step, far_step)))
+                def _():
+                    v.serve(unit)
+
+            @pl.when(step == n)
+            def _():
+                v.side_serve(2)
+
+            @pl.when(step + 1 < steps)
+            def _():
+                for copy in tile_copies(step + 1):
+                    copy.start()
+
+            @pl.when((m == 0) & (step < whole + units))
+            def _():
+                first, second = unit_slots(u)
+
+                @pl.when(jnp.logical_not(diagonal) & (jnp.logical_not(relays) | (u == 2) | (u == 4)))
+                def _():
+                    v.wait_col(first)
+                    v.wait_col(second)
+
+                cols = jnp.concatenate([buf[v.at + base + first], buf[v.at + base + second]], axis=0)
+                width = cols.shape[0]
+                high, low = split(cols)
+                plain[keep, 0:width, :] = high
+                plain[keep, width : 2 * width, :] = high
+                plain[keep, 2 * width : 3 * width, :] = low
+                turned = cols.T
+                for t in range(times):
+                    high, low = split(turned * turned_weight[:, t : t + 1])
+                    weighted[keep, t, 0:depth, :] = high
+                    weighted[keep, t, depth : 2 * depth, :] = high
+                    weighted[keep, t, 2 * depth : 3 * depth, :] = low
+
+            for copy in tile_copies(step):
+                copy.wait()
+            tile = tile_of(m)
+            left = rows[pl.ds(pl.multiple_of(tile * points, chunk), points), :]
+            left = jnp.concatenate([left, left[:, 0:depth]], axis=1)
+            mixed = None
+            for t in range(times):
+                green = jnp.dot(left, weighted[keep, t], preferred_element_type=jnp.float32)
+                term = green * tiles[step % 2, t]
+                mixed = term if mixed is None else mixed + term
+            high, low = split(mixed)
+            mixed = jnp.concatenate([high, low, high], axis=1)
+            acc[tile] = jnp.where(u == 0, 0.0, acc[tile]) + jnp.dot(mixed, plain[keep], preferred_element_type=jnp.float32)
+
+            @pl.when((u == units - 1) & (m == 0))
+            def _():
+                v.partner_sum(0).start()
+
+            @pl.when((u == units - 1) & (m == 1))
+            def _():
+                v.partner_sum(0).wait_recv()
+                for i in range(pieces):
+                    part = slice(i * chunk, (i + 1) * chunk)
+                    acc[twin, part, :] = acc[twin, part, :] + from_partner[2 * p, part, :]
+                    v.twin_sum(i).start()
+
+            @pl.when((u == units - 1) & (m == 2))
+            def _():
+                v.partner_sum(1).start()
+
+        for i in range(pieces):
+            v.to_twin(i).wait_send()
+            v.to_partner(i).wait_send()
+            v.relay(i).wait_send()
+
+        for i in range(1, pieces):
+            for e in range(2):
+                @pl.when(side_goes_down(e))
+                def _():
+                    v.side_down(e, i).wait_send()
+
+                @pl.when(side_goes_up(e))
+                def _():
+                    v.side_up(e, i).wait_send()
+
+                @pl.when(r != side_set(e))
+                def _():
+                    v.side_cross(e, i).wait_send()
+
+        for u in (0, 1, 3, 5):
+            for q in unit_slots(u):
+                @pl.when(goes_down)
+                def _():
+                    v.down(q).wait_send()
+
+                @pl.when(goes_up)
+                def _():
+                    v.up(q).wait_send()
+
+        v.partner_sum(1).wait_recv()
+        for i in range(pieces):
+            part = slice(i * chunk, (i + 1) * chunk)
+            mine = acc[c, part, :] + from_partner[2 * p + 1, part, :]
+            v.twin_sum(i).wait_recv()
+            updated = buf[v.at + c * pieces + i] - (mine + from_twin[p, part, :])
+
+            @pl.when(p == passes - 1)
+            def _():
+                out_ref[part, :] = updated
+
+            @pl.when(p < passes - 1)
+            def _():
+                later = moves(p + 1)
+                buf[later.at + c * pieces + i] = updated
+                later.launch(i)
+
+        for i in range(pieces):
+            v.twin_sum(i).wait_send()
+        for j in range(2):
+            v.partner_sum(j).wait_send()
+
+
+def chain_passes(orbitals, weight, screened):
+    times, n_rows, n_cols = screened.shape
+    points, depth = orbitals.shape
+    n = n_rows // points
+    pieces = 3
+    chunk = points // pieces
+    slots = n * pieces
+    sides = 2 * (pieces - 1)
+    weight = jnp.pad(weight, ((0, -times % 8), (0, 0)))
+    dma = pltpu.SemaphoreType.DMA
+    return pl.pallas_call(
+        functools.partial(chain_kernel, PASSES, times),
+        out_shape=jax.ShapeDtypeStruct((points, depth), jnp.float32),
+        in_specs=[
+            pl.BlockSpec(memory_space=pl.ANY),
+            pl.BlockSpec(memory_space=pltpu.VMEM),
+            pl.BlockSpec(memory_space=pl.ANY),
+        ],
+        out_specs=pl.BlockSpec(memory_space=pltpu.VMEM),
+        scratch_shapes=[
+            pltpu.VMEM((PASSES * (2 * slots + sides), chunk, depth), jnp.float32),
+            pltpu.VMEM((n_rows, 2 * depth), jnp.bfloat16),
+            pltpu.VMEM((pieces, times, 3 * depth, 2 * chunk), jnp.bfloat16),
+            pltpu.VMEM((pieces, 6 * chunk, depth), jnp.bfloat16),
+            pltpu.VMEM((n, points, depth), jnp.float32),
+            pltpu.VMEM((PASSES * 2, points, depth), jnp.float32),
+            pltpu.VMEM((PASSES, points, depth), jnp.float32),
+            pltpu.VMEM((2, times, points, 2 * chunk), jnp.float32),
+            pltpu.VMEM((depth, weight.shape[0]), jnp.float32),
+            dma(()), dma((PASSES * slots,)), dma((PASSES * slots,)), dma((PASSES * sides,)),
+            dma((PASSES * 2,)), dma((PASSES * pieces,)), dma((2, 2)),
+            dma((pieces,)), dma((pieces,)), dma((pieces,)), dma((slots,)), dma((slots,)),
+            dma((sides,)), dma((sides,)), dma((sides,)), dma((2,)), dma((pieces,)),
+        ],
+        compiler_params=pltpu.CompilerParams(
+            collective_id=0, has_side_effects=True, vmem_limit_bytes=60 * 1024 * 1024
+        ),
+        cost_estimate=pl.CostEstimate(
+            flops=PASSES * 6 * (times + 1) * n_rows * n_cols * depth,
+            bytes_accessed=PASSES * 4 * times * n_rows * n_cols,
+            transcendentals=0,
+        ),
+    )(orbitals.reshape(pieces, chunk, depth), weight, screened)
+
+
 def scatter_rows(value):
     n_col = lax.axis_size("col")
     if n_col & (n_col - 1):
@@ -122,6 +546,8 @@
     factor = n_col // n_row
     points, depth = orbitals.shape
     weight = green_weight * time_weight[:, None]
+    if n_row == 4 and n_col == 4 and points % 3 == 0 and (points // 3) % LANES == 0:
+        return chain_passes(orbitals, weight, screened)
     to_columns = [
         ((c // factor) * n_col + (c % factor) * n_row + m, m * n_col + c)
         for m in range(n_row)

time: 470 us -> 287 us (0.61); the launches traced: 462 us -> 286 us
  starting transfers between devices: 134 us -> 0 us
  waiting for transfers between devices: 127 us -> 0 us
  Pallas kernels: 170 us -> 282 us
  between operations: 14 us -> 0.01 us
  other arithmetic: 8.12 us -> 0.78 us
  local copies, waits for them, and re-layouts: 8.65 us -> 2.97 us
    ppermute x12 -> x0, starting transfers between devices: 134 us -> none  [the longest x6 130 us: body(): later = [lax.ppermute(p, 'row', ring) for p in piece]]
    pallas_call x8 -> x1, Pallas kernels: 170 us -> 282 us  [chain_passes(): pl.pallas_call(functools.partial(chain_kernel, PASSES, times), out_shape=...]
    ppermute x12 -> x0, waiting for transfers between devices: 88.9 us -> none  [the longest x4 65.4 us: scatter_rows(): value = mine + lax.ppermute(theirs, 'col', swap)]
    all_gather x2 -> x0, waiting for transfers between devices: 37.2 us -> none  [body(): rows = [lax.all_gather(o, 'col', axis=0, tiled=True) for o in own]]
    squeeze x4 -> x0, local copies, waits for them, and re-layouts: 4.97 us -> none  [scatter_rows(): theirs = lax.dynamic_index_in_dim(pairs, 1 - bit, 1, keepdims=False)]
  transfers between devices with their start and end apart: 14 -> 0, of which waited for: 10 -> 0; matrix products, arithmetic and copies ran while one was open for 0% -> 0% of each run, Pallas kernels for 28% -> 0%
where the time goes in v3:
time: 287 us; the launch traced here: 286 us
  Pallas kernels  282 us (98%)
  local copies, waits for them, and re-layouts  2.97 us (1%)
    pallas_call x1, Pallas kernels, chain_passes(): pl.pallas_call(functools.partial(chain_kernel, PASSES, times), out_shape=...  282 us

profile of v3, /device:TPU:0, one launch (start us, length us, event | category | flops | bytes accessed | tf_op | source)
XLA Modules:
  0.0 285.8 jit_solution(4897908697914726440)
XLA Ops:
  0.0 0.8 broadcast_multiply_fusion
  0.8 0.6 pad.4.weight_ref
  1.4 282.1 %shard_map.46 = f32[384,768]{1,0:T(8,128)} custom-call(f32[3,128,768]{2,1,0:T(8,128)} %bitcast.1, f32[8,768]{1,0:T(8,128)} %pad.4.weight_ref, f32[3,1536,1536]{2,1,0:T(8,128)} %screened_ref.1), custom_call_target="tpu_custom_call" | custom-call | flops 86973087744 | bytes 56623104 | tf_op jit(solution)/shard_map/pallas_call | solution.py:489
  283.5 2.4 copy.6
